TPU v7x, 32 devices: a whole 2x2x4 slice. The times are simulated.
32 devices in a mesh: dp: 4 (over y, x), feat: 8 (over z, core).
Axes of the slice: x: 2, y: 2, z: 4, core: 2. Of those that a mesh axis runs over, the one named last changes fastest.
Arguments:
- sketches: bfloat16 [4, 256, 65536], P('dp', None, 'feat'), may hold values from -24 to 24
Outputs:
- merged: bfloat16 [4, 256, 65536], P('dp', None, 'feat')
All inputs are finite; a program needn't handle non-finite values.
Results may differ from a plain program's by a relative error of at most 0.001.
The roundings to bfloat16 on the way count: a program that leaves them out, or rounds other values in their place, can miss the bound.
Values may be sent and summed in bfloat16 or wider, within the bound.
No kernel may reach another device: no remote copies, remote signals or barrier semaphores. Data moves between devices by JAX's collectives and lax.ppermute only.
A program may use at most 128 MiB of HBM per device.

v0:
```python
import jax
import jax.numpy as jnp
from jax import lax
from jax.sharding import PartitionSpec as P

LEVELS = 2


def from_partner(block, axis, stride):
    count = lax.axis_size(axis)
    route = []
    for low in range(count):
        high = low | 1 << stride
        if high != low and high < count:
            route += [(low, high), (high, low)]
    return lax.ppermute(block, axis, route)


def solve_rows(gram, count):
    size = gram.shape[0]
    average = jnp.trace(gram) / size
    kernel = jnp.eye(size, dtype=jnp.float32) + gram / average
    factor = jnp.linalg.cholesky(kernel)
    target = jnp.eye(size, count, dtype=jnp.float32)
    middle = lax.linalg.triangular_solve(factor, target, left_side=True, lower=True)
    inverse = lax.linalg.triangular_solve(
        factor, middle, left_side=True, lower=True, transpose_a=True
    )
    return inverse.T.astype(jnp.bfloat16)


def per_device(sketches):
    current = sketches[0]
    count = current.shape[0]
    position = lax.axis_index("dp")
    for level in range(LEVELS):
        is_lower = position // 2**level % 2 == 0
        partner = from_partner(current, "dp", level)
        lower = jnp.where(is_lower, current, partner)
        upper = jnp.where(is_lower, partner, current)
        stacked = jnp.concatenate([lower, upper], axis=0)
        partial_gram = jnp.dot(stacked, stacked.T, preferred_element_type=jnp.float32)
        gram_total = lax.psum(partial_gram, "feat")
        weights = solve_rows(gram_total, count)
        update = jnp.dot(weights, stacked, preferred_element_type=jnp.float32)
        fresh = (lower.astype(jnp.float32) - update).astype(jnp.bfloat16)
        current = fresh
    return current[None]


def solution(mesh):
    placed = (P("dp", None, "feat"),)
    return jax.shard_map(
        per_device, mesh=mesh, in_specs=placed, out_specs=P("dp", None, "feat"), check_vma=False
    )
```

profile of v0, /device:TPU:0, one launch (start us, length us, event | category | flops | bytes accessed | tf_op | source)
XLA Modules:
  0.0 661.4 jit_solution(7594506524148744572)
XLA Ops:
  6.5 3.0 collective-permute-start
  9.5 90.9 %collective-permute-done = bf16[256,8192]{1,0:T(8,128)(2,1)} collective-permute-done((bf16[256,8192]{1,0:T(8,128)(2,1)}, bf16[256,8192]{1,0:T(8,128)(2,1)}, u32[]{:S(2)}, u32[]{:S(2)}) %collective-permute-start) | collective-permute-done | bytes 4194336 | tf_op jit(solution)/shard_map/ppermute | solution.py:16
  100.4 5.1 broadcast_select_fusion
  107.4 9.1 %fusion.4 = f32[512,512]{0,1:T(8,128)} fusion(bf16[256,8192]{1,0:T(8,128)(2,1)S(1)} %get-tuple-element.62, bf16[256,8192]{1,0:T(8,128)(2,1)} %get-tuple-element.63), kind=kOutput, calls=%fused_computation.12 | convolution fusion | flops 4311744512 | bytes 9437184 | tf_op jit(solution)/shard_map/dot_general | solution.py:42
  117.1 60.3 %all-reduce.4.cloned.1.call-done = f32[512,512]{0,1:T(8,128)} async-done(((f32[512,512]{0,1:T(8,128)}), f32[512,512]{0,1:T(8,128)}) %all-reduce.4.cloned.1.call-update) | async-done | bytes 1048592 | tf_op jit(solution)/shard_map/psum | solution.py:43
  177.4 2.0 select_reduce_fusion.1
  185.2 11.7 %cholesky.286 = f32[128,128]{1,0:T(8,128)S(1)} custom-call(f32[128,128]{1,0:T(8,128)S(1)} %cholesky.426), custom_call_target="Cholesky" | custom-call | tf_op jit(solution)/shard_map/jit(cholesky)/cholesky | solution.py:23
  197.1 9.8 %custom-call.31 = f32[1,128,128]{1,2,0:T(8,128)S(1)} custom-call(f32[1,128,128]{2,1,0:T(8,128)S(1)} %get-tuple-element.83), custom_call_target="InvertDiagBlocksLowerTriangular" | custom-call | tf_op jit(solution)/shard_map/jit(cholesky)/cholesky | solution.py:23
  209.4 11.7 %cholesky.305 = f32[128,128]{1,0:T(8,128)S(1)} custom-call(f32[128,128]{1,0:T(8,128)S(1)} %cholesky.430), custom_call_target="Cholesky" | custom-call | tf_op jit(solution)/shard_map/jit(cholesky)/cholesky | solution.py:23
  221.2 10.0 %custom-call.32 = f32[1,128,128]{1,2,0:T(8,128)S(1)} custom-call(f32[1,128,128]{2,1,0:T(8,128)S(1)} %get-tuple-element.80), custom_call_target="InvertDiagBlocksLowerTriangular" | custom-call | tf_op jit(solution)/shard_map/jit(cholesky)/cholesky | solution.py:23
  232.7 11.7 %cholesky.326 = f32[128,128]{1,0:T(8,128)S(1)} custom-call(f32[128,128]{1,0:T(8,128)S(1)} %cholesky.435), custom_call_target="Cholesky" | custom-call | tf_op jit(solution)/shard_map/jit(cholesky)/cholesky | solution.py:23
  245.1 9.8 %custom-call.33 = f32[1,128,128]{1,2,0:T(8,128)S(1)} custom-call(f32[1,128,128]{2,1,0:T(8,128)S(1)} %get-tuple-element.77), custom_call_target="InvertDiagBlocksLowerTriangular" | custom-call | tf_op jit(solution)/shard_map/jit(cholesky)/cholesky | solution.py:23
  256.4 11.9 %cholesky.343 = f32[128,128]{1,0:T(8,128)S(1)} custom-call(f32[128,128]{1,0:T(8,128)S(1)} %convolution_subtract_fusion.17), custom_call_target="Cholesky" | custom-call | tf_op jit(solution)/shard_map/jit(cholesky)/cholesky | solution.py:23
  272.4 8.1 %while.8 = (s32[]{:T(128)}, f32[512,512]{1,0:T(8,128)S(1)}, s32[4,2]{0,1:T(2,128)S(1)}, f32[4,128,128]{2,1,0:T(8,128)S(1)}, s32[]{:T(128)}) while((s32[]{:T(128)}, f32[512,512]{1,0:T(8,128)S(1)}, s32[4,2]{0,1:T(2,128)S(1)}, f32[4,128,128]{2,1,0:T(8,128)S(1)}, s32[]{:T(128)}) %tuple.61), condition=%wide.while_cond.1, body=%wide.while_body.1.sunk | while | flops 2 | bytes 131181 | solution.py:26
  280.6 39.3 %custom-call.35 = f32[4,128,128]{1,2,0:T(8,128)S(1)} custom-call(f32[4,128,128]{2,1,0:T(8,128)S(1)} %get-tuple-element.37), custom_call_target="InvertDiagBlocksLowerTriangular" | custom-call | tf_op jit(solution)/shard_map/triangular_solve/custom-call.8 | solution.py:26
  324.4 8.1 %subtract_convert_fusion.1 = bf16[256,8192]{1,0:T(8,128)(2,1)} fusion(bf16[256,8192]{1,0:T(8,128)(2,1)} %get-tuple-element.63, bf16[256,8192]{1,0:T(8,128)(2,1)S(1)} %copy-done.3, f32[128,256]{1,0:T(8,128)S(1)} %fusion.84, f32[128,256]{1,0:T(8,128)S(1)} %fusion.82, f32[128,256]{1,0:T(8,128)S(1)} %fusion.80, bf16[128,256]{1,0:T(8,128)(2,1)S(1)} %fusion.78), kind=kOutput, calls=%fused_computation.7 | convolution fusion | flops 2171600896 | bytes 13041664 | tf_op jit(solution)/shard_map/dot_general | solution.py:45
  334.0 89.4 %collective-permute-done.1 = bf16[256,8192]{1,0:T(8,128)(2,1)} collective-permute-done((bf16[256,8192]{1,0:T(8,128)(2,1)}, bf16[256,8192]{1,0:T(8,128)(2,1)}, u32[]{:S(2)}, u32[]{:S(2)}) %collective-permute-start.1) | collective-permute-done | bytes 4194336 | tf_op jit(solution)/shard_map/ppermute | solution.py:16
  423.4 5.5 broadcast_select_fusion.3
  428.9 2.0 copy-done.4
  430.9 9.0 %fusion.1 = f32[512,512]{0,1:T(8,128)} fusion(bf16[256,8192]{1,0:T(8,128)(2,1)} %get-tuple-element.61, bf16[256,8192]{1,0:T(8,128)(2,1)S(1)} %get-tuple-element.60), kind=kOutput, calls=%fused_computation.9 | convolution fusion | flops 4311744512 | bytes 9437184 | tf_op jit(solution)/shard_map/dot_general | solution.py:42
  440.0 59.3 %all-reduce.6.cloned.1.call-done = f32[512,512]{0,1:T(8,128)} async-done(((f32[512,512]{0,1:T(8,128)}), f32[512,512]{0,1:T(8,128)}) %all-reduce.6.cloned.1.call-update) | async-done | bytes 1048592 | tf_op jit(solution)/shard_map/psum | solution.py:43
  499.2 2.1 select_reduce_fusion
  507.2 11.7 %cholesky.358 = f32[128,128]{1,0:T(8,128)S(1)} custom-call(f32[128,128]{1,0:T(8,128)S(1)} %cholesky.439), custom_call_target="Cholesky" | custom-call | tf_op jit(solution)/shard_map/jit(cholesky)/cholesky | solution.py:23
  519.1 9.8 %custom-call.36 = f32[1,128,128]{1,2,0:T(8,128)S(1)} custom-call(f32[1,128,128]{2,1,0:T(8,128)S(1)} %get-tuple-element.73), custom_call_target="InvertDiagBlocksLowerTriangular" | custom-call | tf_op jit(solution)/shard_map/jit(cholesky)/cholesky | solution.py:23
  531.4 11.9 %cholesky.377 = f32[128,128]{1,0:T(8,128)S(1)} custom-call(f32[128,128]{1,0:T(8,128)S(1)} %cholesky.443), custom_call_target="Cholesky" | custom-call | tf_op jit(solution)/shard_map/jit(cholesky)/cholesky | solution.py:23
  544.7 9.8 %custom-call.37 = f32[1,128,128]{1,2,0:T(8,128)S(1)} custom-call(f32[1,128,128]{2,1,0:T(8,128)S(1)} %get-tuple-element.70), custom_call_target="InvertDiagBlocksLowerTriangular" | custom-call | tf_op jit(solution)/shard_map/jit(cholesky)/cholesky | solution.py:23
  556.0 11.7 %cholesky.398 = f32[128,128]{1,0:T(8,128)S(1)} custom-call(f32[128,128]{1,0:T(8,128)S(1)} %cholesky.448), custom_call_target="Cholesky" | custom-call | tf_op jit(solution)/shard_map/jit(cholesky)/cholesky | solution.py:23
  568.5 9.8 %custom-call.38 = f32[1,128,128]{1,2,0:T(8,128)S(1)} custom-call(f32[1,128,128]{2,1,0:T(8,128)S(1)} %get-tuple-element.67), custom_call_target="InvertDiagBlocksLowerTriangular" | custom-call | tf_op jit(solution)/shard_map/jit(cholesky)/cholesky | solution.py:23
  579.9 11.7 %cholesky.415 = f32[128,128]{1,0:T(8,128)S(1)} custom-call(f32[128,128]{1,0:T(8,128)S(1)} %convolution_subtract_fusion.16), custom_call_target="Cholesky" | custom-call | tf_op jit(solution)/shard_map/jit(cholesky)/cholesky | solution.py:23
  595.1 8.1 %while.9 = (s32[]{:T(128)}, f32[512,512]{1,0:T(8,128)S(1)}, s32[4,2]{0,1:T(2,128)S(1)}, f32[4,128,128]{2,1,0:T(8,128)S(1)}, s32[]{:T(128)}) while((s32[]{:T(128)}, f32[512,512]{1,0:T(8,128)S(1)}, s32[4,2]{0,1:T(2,128)S(1)}, f32[4,128,128]{2,1,0:T(8,128)S(1)}, s32[]{:T(128)}) %tuple.71), condition=%wide.while_cond.1.clone, body=%wide.while_body.1.clone.sunk | while | flops 2 | bytes 131181 | solution.py:26
  603.3 39.6 %custom-call.40 = f32[4,128,128]{1,2,0:T(8,128)S(1)} custom-call(f32[4,128,128]{2,1,0:T(8,128)S(1)} %get-tuple-element.39), custom_call_target="InvertDiagBlocksLowerTriangular" | custom-call | tf_op jit(solution)/shard_map/triangular_solve/custom-call.8 | solution.py:26
  647.4 6.8 %fusion.2 = bf16[1,256,8192]{2,1,0:T(8,128)(2,1)} fusion(bf16[256,8192]{1,0:T(8,128)(2,1)} %get-tuple-element.61, bf16[256,8192]{1,0:T(8,128)(2,1)S(1)} %copy-done.5, f32[128,256]{1,0:T(8,128)S(1)} %fusion.91, f32[128,256]{1,0:T(8,128)S(1)} %fusion.89, f32[128,256]{1,0:T(8,128)S(1)} %fusion.87, bf16[128,256]{1,0:T(8,128)(2,1)S(1)} %fusion.85), kind=kOutput, calls=%fused_computation.10 | convolution fusion | flops 2171600896 | bytes 13041664 | tf_op jit(solution)/shard_map/dot_general | solution.py:45
  (120 shorter events, 56.1 us)
Async XLA Ops:
  6.5 170.9 %all-reduce.4.cloned.1.call-start = ((), (), s32[]{:S(2)}) async-start(), calls=%async_computation | async-start | bytes 2097152 | tf_op jit(solution)/shard_map/psum | solution.py:43
  6.5 93.9 %collective-permute-start = (bf16[256,8192]{1,0:T(8,128)(2,1)}, bf16[256,8192]{1,0:T(8,128)(2,1)}, u32[]{:S(2)}, u32[]{:S(2)}) collective-permute-start(bf16[256,8192]{1,0:T(8,128)(2,1)} %bitcast.133), channel_id=1, source_target_pairs={{0,8},{8,0},{16,24},{24,16},{1,9},{9,1},{17,25},{25,17},{2,10},{10... | collective-permute-start | bytes 12582920 | tf_op jit(solution)/shard_map/ppermute | solution.py:16
  105.5 1.9 copy-start.2
  116.5 382.7 %all-reduce.6.cloned.1.call-start = ((), (), s32[]{:S(2)}) async-start(), calls=%async_computation.1 | async-start | bytes 2097152 | tf_op jit(solution)/shard_map/psum | solution.py:43
  177.4 5.4 copy-start
  184.2 1.0 copy-start.7
  319.9 4.5 copy-start.3
  332.6 90.8 %collective-permute-start.1 = (bf16[256,8192]{1,0:T(8,128)(2,1)}, bf16[256,8192]{1,0:T(8,128)(2,1)}, u32[]{:S(2)}, u32[]{:S(2)}) collective-permute-start(bf16[256,8192]{1,0:T(8,128)(2,1)} %subtract_convert_fusion.1), channel_id=1, source_target_pairs={{0,16},{16,0},{8,24},{24,8},{1,17},{17,1},{9,25},{25,9},{2,18},{18... | collective-permute-start | bytes 12582920 | tf_op jit(solution)/shard_map/ppermute | solution.py:16
  428.9 2.0 copy-start.4
  499.2 5.5 copy-start.1
  506.2 1.0 copy-start.6
  642.9 4.5 copy-start.5
Sparse Core Ops, SparseCore 0:
  116.6 60.7 all-reduce.3
  440.1 59.1 all-reduce.5
where the time goes:
time: 666 us; the launch traced here: 661 us
  waiting for transfers between devices  300 us (45%)
  other arithmetic  258 us (39%)
  matrix products  53 us (8%)
  local copies, waits for them, and re-layouts  25.1 us (4%)
  between operations  20.7 us (3%)
    ppermute x2, waiting for transfers between devices, from_partner(): return lax.ppermute(block, axis, route)  180 us
    another operation x29, other arithmetic, solve_rows(): factor = jnp.linalg.cholesky(kernel)  158 us
    psum x2, waiting for transfers between devices, per_device(): gram_total = lax.psum(partial_gram, 'feat')  120 us
    another operation x5, other arithmetic, solve_rows(): lax.linalg.triangular_solve(factor, middle, left_side=True, lower=True, t...  79.1 us
    dot_general x2, matrix products, per_device(): jnp.dot(stacked, stacked.T, preferred_element_type=jnp.float32)  18.1 us
    another operation x27, local copies, waits for them, and re-layouts, solve_rows(): lax.linalg.triangular_solve(factor, middle, left_side=True, lower=True, t...  16.1 us
    dot_general x2, matrix products, per_device(): update = jnp.dot(weights, stacked, preferred_element_type=jnp.float32)  15 us
  transfers between devices with their start and end apart: 4, of which 4 were waited for; matrix products, arithmetic and copies ran while one was open for 0% of the time, Pallas kernels for 0%

commit v1 on v0

--- a/solution.py
+++ b/solution.py
@@ -40,7 +40,7 @@
         upper = jnp.where(is_lower, partner, current)
         stacked = jnp.concatenate([lower, upper], axis=0)
         partial_gram = jnp.dot(stacked, stacked.T, preferred_element_type=jnp.float32)
-        gram_total = lax.psum(partial_gram, "feat")
+        gram_total = jnp.sum(lax.all_gather(partial_gram, "feat"), axis=0)
         weights = solve_rows(gram_total, count)
         update = jnp.dot(weights, stacked, preferred_element_type=jnp.float32)
         fresh = (lower.astype(jnp.float32) - update).astype(jnp.bfloat16)

time: 666 us -> 717 us (1.077)
  waiting for transfers between devices: 300 us -> 346 us
    all_gather x0 -> x2, waiting for transfers between devices: none -> 164 us  [per_device(): gram_total = jnp.sum(lax.all_gather(partial_gram, 'feat'), axis=0)]
    psum x2 -> x0, waiting for transfers between devices: 120 us -> none  [per_device(): gram_total = lax.psum(partial_gram, 'feat')]
    reduce_sum x0 -> x2, other arithmetic: none -> 8.98 us  [per_device(): gram_total = jnp.sum(lax.all_gather(partial_gram, 'feat'), axis=0)]
where the time goes in v1:
time: 717 us; the launch traced here: 712 us
  waiting for transfers between devices  346 us (48%)
  other arithmetic  262 us (37%)
  matrix products  52.9 us (7%)
  local copies, waits for them, and re-layouts  25.8 us (4%)
  between operations  20.7 us (3%)
    ppermute x2, waiting for transfers between devices, from_partner(): return lax.ppermute(block, axis, route)  182 us
    all_gather x2, waiting for transfers between devices, per_device(): gram_total = jnp.sum(lax.all_gather(partial_gram, 'feat'), axis=0)  164 us
    another operation x29, other arithmetic, solve_rows(): factor = jnp.linalg.cholesky(kernel)  158 us
    another operation x5, other arithmetic, solve_rows(): lax.linalg.triangular_solve(factor, middle, left_side=True, lower=True, t...  79.1 us
    dot_general x2, matrix products, per_device(): jnp.dot(stacked, stacked.T, preferred_element_type=jnp.float32)  18.1 us
    another operation x27, local copies, waits for them, and re-layouts, solve_rows(): lax.linalg.triangular_solve(factor, middle, left_side=True, lower=True, t...  16.2 us
    dot_general x2, matrix products, per_device(): update = jnp.dot(weights, stacked, preferred_element_type=jnp.float32)  15 us
  transfers between devices with their start and end apart: 4, of which 4 were waited for; matrix products, arithmetic and copies ran while one was open for 0% of the time, Pallas kernels for 0%

profile of v1, /device:TPU:0, one launch (start us, length us, event | category | flops | bytes accessed | tf_op | source)
XLA Modules:
  0.0 712.4 jit_solution(3782523139644673443)
XLA Ops:
  6.5 3.0 collective-permute-start
  9.5 90.9 %collective-permute-done = bf16[256,8192]{1,0:T(8,128)(2,1)} collective-permute-done((bf16[256,8192]{1,0:T(8,128)(2,1)}, bf16[256,8192]{1,0:T(8,128)(2,1)}, u32[]{:S(2)}, u32[]{:S(2)}) %collective-permute-start) | collective-permute-done | bytes 4194336 | tf_op jit(solution)/shard_map/ppermute | solution.py:16
  100.4 5.1 broadcast_select_fusion
  107.4 9.1 %fusion.4 = f32[512,512]{1,0:T(8,128)} fusion(bf16[256,8192]{1,0:T(8,128)(2,1)S(1)} %get-tuple-element.62, bf16[256,8192]{1,0:T(8,128)(2,1)} %get-tuple-element.63), kind=kOutput, calls=%fused_computation.12 | convolution fusion | flops 4311744512 | bytes 9437184 | tf_op jit(solution)/shard_map/dot_general | solution.py:42
  117.2 83.1 %all-gather.5.cloned.1.call-done = f32[4096,512]{1,0:T(8,128)} async-done(((f32[512,512]{1,0:T(8,128)}), f32[4096,512]{1,0:T(8,128)}) %all-gather.5.cloned.1.call-update) | async-done | bytes 8388624 | tf_op jit(solution)/shard_map/all_gather | solution.py:43
  200.3 4.5 reduce_sum.34
  210.3 11.7 %cholesky.286 = f32[128,128]{1,0:T(8,128)S(1)} custom-call(f32[128,128]{1,0:T(8,128)S(1)} %cholesky.426), custom_call_target="Cholesky" | custom-call | tf_op jit(solution)/shard_map/jit(cholesky)/cholesky | solution.py:23
  222.2 9.8 %custom-call.31 = f32[1,128,128]{1,2,0:T(8,128)S(1)} custom-call(f32[1,128,128]{2,1,0:T(8,128)S(1)} %get-tuple-element.83), custom_call_target="InvertDiagBlocksLowerTriangular" | custom-call | tf_op jit(solution)/shard_map/jit(cholesky)/cholesky | solution.py:23
  234.5 11.9 %cholesky.305 = f32[128,128]{1,0:T(8,128)S(1)} custom-call(f32[128,128]{1,0:T(8,128)S(1)} %cholesky.430), custom_call_target="Cholesky" | custom-call | tf_op jit(solution)/shard_map/jit(cholesky)/cholesky | solution.py:23
  246.4 9.8 %custom-call.32 = f32[1,128,128]{1,2,0:T(8,128)S(1)} custom-call(f32[1,128,128]{2,1,0:T(8,128)S(1)} %get-tuple-element.80), custom_call_target="InvertDiagBlocksLowerTriangular" | custom-call | tf_op jit(solution)/shard_map/jit(cholesky)/cholesky | solution.py:23
  257.8 11.7 %cholesky.326 = f32[128,128]{1,0:T(8,128)S(1)} custom-call(f32[128,128]{1,0:T(8,128)S(1)} %cholesky.435), custom_call_target="Cholesky" | custom-call | tf_op jit(solution)/shard_map/jit(cholesky)/cholesky | solution.py:23
  270.3 9.8 %custom-call.33 = f32[1,128,128]{1,2,0:T(8,128)S(1)} custom-call(f32[1,128,128]{2,1,0:T(8,128)S(1)} %get-tuple-element.77), custom_call_target="InvertDiagBlocksLowerTriangular" | custom-call | tf_op jit(solution)/shard_map/jit(cholesky)/cholesky | solution.py:23
  281.5 11.9 %cholesky.343 = f32[128,128]{1,0:T(8,128)S(1)} custom-call(f32[128,128]{1,0:T(8,128)S(1)} %convolution_subtract_fusion.17), custom_call_target="Cholesky" | custom-call | tf_op jit(solution)/shard_map/jit(cholesky)/cholesky | solution.py:23
  297.6 8.2 %while.8 = (s32[]{:T(128)}, f32[512,512]{1,0:T(8,128)S(1)}, s32[4,2]{0,1:T(2,128)S(1)}, f32[4,128,128]{2,1,0:T(8,128)S(1)}, s32[]{:T(128)}) while((s32[]{:T(128)}, f32[512,512]{1,0:T(8,128)S(1)}, s32[4,2]{0,1:T(2,128)S(1)}, f32[4,128,128]{2,1,0:T(8,128)S(1)}, s32[]{:T(128)}) %tuple.61), condition=%wide.while_cond.1, body=%wide.while_body.1.sunk | while | flops 2 | bytes 131181 | solution.py:26
  305.8 39.3 %custom-call.35 = f32[4,128,128]{1,2,0:T(8,128)S(1)} custom-call(f32[4,128,128]{2,1,0:T(8,128)S(1)} %get-tuple-element.37), custom_call_target="InvertDiagBlocksLowerTriangular" | custom-call | tf_op jit(solution)/shard_map/triangular_solve/custom-call.8 | solution.py:26
  349.7 8.1 %subtract_convert_fusion.1 = bf16[256,8192]{1,0:T(8,128)(2,1)} fusion(bf16[256,8192]{1,0:T(8,128)(2,1)} %get-tuple-element.63, bf16[256,8192]{1,0:T(8,128)(2,1)S(1)} %copy-done.1, f32[128,256]{1,0:T(8,128)S(1)} %fusion.84, f32[128,256]{1,0:T(8,128)S(1)} %fusion.82, f32[128,256]{1,0:T(8,128)S(1)} %fusion.80, bf16[128,256]{1,0:T(8,128)(2,1)S(1)} %fusion.78), kind=kOutput, calls=%fused_computation.7 | convolution fusion | flops 2171600896 | bytes 13041664 | tf_op jit(solution)/shard_map/dot_general | solution.py:45
  359.3 91.6 %collective-permute-done.1 = bf16[256,8192]{1,0:T(8,128)(2,1)} collective-permute-done((bf16[256,8192]{1,0:T(8,128)(2,1)}, bf16[256,8192]{1,0:T(8,128)(2,1)}, u32[]{:S(2)}, u32[]{:S(2)}) %collective-permute-start.1) | collective-permute-done | bytes 4194336 | tf_op jit(solution)/shard_map/ppermute | solution.py:16
  450.9 5.4 broadcast_select_fusion.3
  456.3 2.0 copy-done.2
  458.3 9.0 %fusion.1 = f32[512,512]{1,0:T(8,128)} fusion(bf16[256,8192]{1,0:T(8,128)(2,1)} %get-tuple-element.61, bf16[256,8192]{1,0:T(8,128)(2,1)S(1)} %get-tuple-element.60), kind=kOutput, calls=%fused_computation.9 | convolution fusion | flops 4311744512 | bytes 9437184 | tf_op jit(solution)/shard_map/dot_general | solution.py:42
  467.4 80.7 %all-gather.7.cloned.1.call-done = f32[4096,512]{1,0:T(8,128)} async-done(((f32[512,512]{1,0:T(8,128)}), f32[4096,512]{1,0:T(8,128)}) %all-gather.7.cloned.1.call-update) | async-done | bytes 8388624 | tf_op jit(solution)/shard_map/all_gather | solution.py:43
  548.0 4.5 reduce_sum.36
  558.1 11.7 %cholesky.358 = f32[128,128]{1,0:T(8,128)S(1)} custom-call(f32[128,128]{1,0:T(8,128)S(1)} %cholesky.439), custom_call_target="Cholesky" | custom-call | tf_op jit(solution)/shard_map/jit(cholesky)/cholesky | solution.py:23
  570.0 10.0 %custom-call.36 = f32[1,128,128]{1,2,0:T(8,128)S(1)} custom-call(f32[1,128,128]{2,1,0:T(8,128)S(1)} %get-tuple-element.73), custom_call_target="InvertDiagBlocksLowerTriangular" | custom-call | tf_op jit(solution)/shard_map/jit(cholesky)/cholesky | solution.py:23
  582.5 11.7 %cholesky.377 = f32[128,128]{1,0:T(8,128)S(1)} custom-call(f32[128,128]{1,0:T(8,128)S(1)} %cholesky.443), custom_call_target="Cholesky" | custom-call | tf_op jit(solution)/shard_map/jit(cholesky)/cholesky | solution.py:23
  595.6 9.8 %custom-call.37 = f32[1,128,128]{1,2,0:T(8,128)S(1)} custom-call(f32[1,128,128]{2,1,0:T(8,128)S(1)} %get-tuple-element.70), custom_call_target="InvertDiagBlocksLowerTriangular" | custom-call | tf_op jit(solution)/shard_map/jit(cholesky)/cholesky | solution.py:23
  607.0 11.7 %cholesky.398 = f32[128,128]{1,0:T(8,128)S(1)} custom-call(f32[128,128]{1,0:T(8,128)S(1)} %cholesky.448), custom_call_target="Cholesky" | custom-call | tf_op jit(solution)/shard_map/jit(cholesky)/cholesky | solution.py:23
  619.4 10.0 %custom-call.38 = f32[1,128,128]{1,2,0:T(8,128)S(1)} custom-call(f32[1,128,128]{2,1,0:T(8,128)S(1)} %get-tuple-element.67), custom_call_target="InvertDiagBlocksLowerTriangular" | custom-call | tf_op jit(solution)/shard_map/jit(cholesky)/cholesky | solution.py:23
  630.9 11.7 %cholesky.415 = f32[128,128]{1,0:T(8,128)S(1)} custom-call(f32[128,128]{1,0:T(8,128)S(1)} %convolution_subtract_fusion.16), custom_call_target="Cholesky" | custom-call | tf_op jit(solution)/shard_map/jit(cholesky)/cholesky | solution.py:23
  646.1 8.2 %while.9 = (s32[]{:T(128)}, f32[512,512]{1,0:T(8,128)S(1)}, s32[4,2]{0,1:T(2,128)S(1)}, f32[4,128,128]{2,1,0:T(8,128)S(1)}, s32[]{:T(128)}) while((s32[]{:T(128)}, f32[512,512]{1,0:T(8,128)S(1)}, s32[4,2]{0,1:T(2,128)S(1)}, f32[4,128,128]{2,1,0:T(8,128)S(1)}, s32[]{:T(128)}) %tuple.71), condition=%wide.while_cond.1.clone, body=%wide.while_body.1.clone.sunk | while | flops 2 | bytes 131181 | solution.py:26
  654.3 39.6 %custom-call.40 = f32[4,128,128]{1,2,0:T(8,128)S(1)} custom-call(f32[4,128,128]{2,1,0:T(8,128)S(1)} %get-tuple-element.39), custom_call_target="InvertDiagBlocksLowerTriangular" | custom-call | tf_op jit(solution)/shard_map/triangular_solve/custom-call.8 | solution.py:26
  698.4 6.8 fusion.2
  (120 shorter events, 55.7 us)
Async XLA Ops:
  6.5 193.7 %all-gather.5.cloned.1.call-start = ((), (), s32[]{:S(2)}) async-start(), calls=%async_computation | async-start | bytes 9437184 | tf_op jit(solution)/shard_map/all_gather | solution.py:43
  6.5 93.9 %collective-permute-start = (bf16[256,8192]{1,0:T(8,128)(2,1)}, bf16[256,8192]{1,0:T(8,128)(2,1)}, u32[]{:S(2)}, u32[]{:S(2)}) collective-permute-start(bf16[256,8192]{1,0:T(8,128)(2,1)} %bitcast.137), channel_id=1, source_target_pairs={{0,8},{8,0},{16,24},{24,16},{1,9},{9,1},{17,25},{25,17},{2,10},{10... | collective-permute-start | bytes 12582920 | tf_op jit(solution)/shard_map/ppermute | solution.py:16
  105.5 2.0 copy-start
  116.6 431.5 %all-gather.7.cloned.1.call-start = ((), (), s32[]{:S(2)}) async-start(), calls=%async_computation.1 | async-start | bytes 9437184 | tf_op jit(solution)/shard_map/all_gather | solution.py:43
  209.3 1.0 copy-start.5
  345.1 4.6 copy-start.1
  357.9 93.0 %collective-permute-start.1 = (bf16[256,8192]{1,0:T(8,128)(2,1)}, bf16[256,8192]{1,0:T(8,128)(2,1)}, u32[]{:S(2)}, u32[]{:S(2)}) collective-permute-start(bf16[256,8192]{1,0:T(8,128)(2,1)} %subtract_convert_fusion.1), channel_id=1, source_target_pairs={{0,16},{16,0},{8,24},{24,8},{1,17},{17,1},{9,25},{25,9},{2,18},{18... | collective-permute-start | bytes 12582920 | tf_op jit(solution)/shard_map/ppermute | solution.py:16
  456.3 2.0 copy-start.2
  557.1 1.0 copy-start.4
  693.9 4.5 copy-start.3
Sparse Core Ops, SparseCore 0:
  116.7 83.5 all-gather.4
  467.5 80.5 all-gather.6
